TPU v7x, 32 devices: a whole 2x2x4 slice. The times are simulated.
32 devices in a mesh: gx: 8 (over z, core), gy: 4 (over y, x).
Axes of the slice: x: 2, y: 2, z: 4, core: 2. Of those that a mesh axis runs over, the one named last changes fastest.
Arguments:
- init_re: float32 [1, 256, 4096], P(None, 'gx', 'gy'), may hold values from -6 to 6
- init_im: float32 [1, 256, 4096], P(None, 'gx', 'gy'), may hold values from -6 to 6
- onsite: float32 [256, 4096], P('gx', 'gy'), may hold values from -0.9 to 0.9
- bond_x: int32 [256, 4096], P('gx', 'gy'), may hold values from 0 to 15
- bond_y: int32 [256, 4096], P('gx', 'gy'), may hold values from 0 to 15
- hop_table: float32 [16], replicated, may hold values from 1.4 to 1.6
- centre: int32 [1, 2], replicated, may hold values from 0 to 255
- duration: float32 [1], replicated, may hold values from 0.55 to 0.6
Outputs:
- out_re: float32 [1, 256, 4096], P(None, 'gx', 'gy')
- out_im: float32 [1, 256, 4096], P(None, 'gx', 'gy')
- term_norms: float32 [2, 8, 1], replicated
All inputs are finite; a program needn't handle non-finite values.
Results may differ from a plain program's by a relative error of at most 0.0003.
Values sent between devices are 32-bit elements; how exact they have to be, the bound alone decides.
A program may use at most 64 MiB of HBM per device.

v0:
```python
import math
import jax
import jax.numpy as jnp
from jax import lax
from jax.sharding import PartitionSpec as P

TERMS = 8
STEPS = 2
SPECTRAL = 7.5
epsilon = 1e-06


def padded(block, sides, width):
    for axis, dim in sides:
        count = lax.axis_size(axis)
        forward = [(i, i + 1) for i in range(count - 1)]
        forward.append((count - 1, 0))
        backward = [(target, source) for source, target in forward]
        low = lax.ppermute(
            lax.slice_in_dim(block, block.shape[dim] - width, None, axis=dim), axis, forward
        )
        high = lax.ppermute(lax.slice_in_dim(block, 0, width, axis=dim), axis, backward)
        block = jnp.concatenate([low, block, high], axis=dim)
    return block


def bessel_weights(duration):
    argument = duration[0] * SPECTRAL
    halved = argument * 0.5
    weights = []
    for degree in range(TERMS):
        series = halved**degree / math.factorial(degree)
        summed = series
        for counter in range(1, 24):
            series = series * -(halved * halved) / (counter * (counter + degree))
            summed = summed + series
        weights.append(summed if degree == 0 else 2.0 * summed)
    return weights


def rotated(degree, real_part, imag_part):
    quarter = degree % 4
    if quarter == 0:
        return (real_part, imag_part)
    if quarter == 1:
        return (imag_part, -real_part)
    if quarter == 2:
        return (-real_part, -imag_part)
    return (-imag_part, real_part)


def falloff(positions, centres, extent):
    distance = jnp.mod(positions[None, :] - centres[:, None], extent)
    distance = jnp.minimum(distance, extent - distance).astype(jnp.float32)
    return distance * distance * (4.5 / (extent * extent))


def shrink(tensor, margin):
    if margin == 0:
        return tensor
    return tensor[..., margin : tensor.shape[-2] - margin, margin : tensor.shape[-1] - margin]


def apply_wide(grid_field, coeffs):
    potential = coeffs[0]
    hop_rows = coeffs[1]
    hop_cols = coeffs[2]
    result = potential[1:-1, 1:-1] * grid_field[..., 1:-1, 1:-1]
    result = result - hop_rows[1:-1, 1:-1] * grid_field[..., 2:, 1:-1]
    result = result - hop_rows[:-2, 1:-1] * grid_field[..., :-2, 1:-1]
    result = result - hop_cols[1:-1, 1:-1] * grid_field[..., 1:-1, 2:]
    result = result - hop_cols[1:-1, :-2] * grid_field[..., 1:-1, :-2]
    return result * (1.0 / SPECTRAL)


def per_device(init_re, init_im, onsite, bond_x, bond_y, hop_table, centre, duration):
    packets, rows_local, cols_local = init_re.shape
    rows_total = rows_local * lax.axis_size("gx")
    cols_total = cols_local * lax.axis_size("gy")
    cell_count = rows_total * cols_total
    classes = hop_table.shape[0]
    selector = jnp.arange(classes, dtype=jnp.int32)[:, None, None]
    table_column = hop_table[:, None, None]
    hop_down = jnp.sum(jnp.where(bond_x[None] == selector, table_column, 0.0), axis=0)
    hop_right = jnp.sum(jnp.where(bond_y[None] == selector, table_column, 0.0), axis=0)
    weights = bessel_weights(duration)
    row_index = lax.axis_index("gx") * rows_local + lax.iota(jnp.int32, rows_local)
    col_index = lax.axis_index("gy") * cols_local + lax.iota(jnp.int32, cols_local)
    row_fall = falloff(row_index, centre[:, 0], rows_total)
    col_fall = falloff(col_index, centre[:, 1], cols_total)
    envelope = jnp.exp(-(row_fall[:, :, None] + col_fall[:, None, :]))
    packet_state = jnp.stack([init_re * envelope, init_im * envelope])
    reach = TERMS - 1
    coeffs = padded(jnp.stack([onsite, hop_down, hop_right]), (("gx", 1), ("gy", 2)), reach)
    norm_rows = []
    for repeat in range(STEPS):
        current = padded(packet_state, (("gx", 2), ("gy", 3)), reach)
        margin = reach
        previous = current
        previous_margin = reach
        chebyshev = [packet_state]
        for chebyshev_degree in range(1, TERMS):
            applied = apply_wide(current, shrink(coeffs, reach - margin))
            if chebyshev_degree == 1:
                following = applied
            else:
                following = 2.0 * applied - shrink(previous, previous_margin - margin + 1)
            previous, previous_margin = (current, margin)
            current = following
            margin = margin - 1
            chebyshev.append(shrink(following, margin))
        accumulate = weights[0] * packet_state
        for degree in range(1, TERMS):
            real_rot, imag_rot = rotated(degree, chebyshev[degree][0], chebyshev[degree][1])
            accumulate = accumulate + weights[degree] * jnp.stack([real_rot, imag_rot])
        term_local = jnp.stack([jnp.sum(vector * vector, axis=(0, 2, 3)) for vector in chebyshev])
        state_local = jnp.sum(accumulate * accumulate, axis=(0, 2, 3))
        term_total, state_total = lax.psum((term_local, state_local), ("gx", "gy"))
        norm_rows.append(term_total / cell_count)
        rescale = lax.rsqrt(state_total / cell_count + epsilon)
        packet_state = accumulate * rescale[None, :, None, None]
    return (packet_state[0], packet_state[1], jnp.stack(norm_rows))


def solution(mesh):
    return jax.shard_map(
        per_device,
        mesh=mesh,
        in_specs=(
            P(None, "gx", "gy"),
            P(None, "gx", "gy"),
            P("gx", "gy"),
            P("gx", "gy"),
            P("gx", "gy"),
            P(),
            P(),
            P(),
        ),
        out_specs=(P(None, "gx", "gy"), P(None, "gx", "gy"), P()),
        check_vma=False,
    )
```

profile of v0, /device:TPU:0, one launch (start us, length us, event | category | flops | bytes accessed | tf_op | source)
XLA Modules:
  0.0 153.5 jit_solution(4384548073286884623)
XLA Ops:
  0.7 1.3 fusion.128
  2.0 0.7 fusion.100
  2.6 0.7 fusion.97
  3.3 1.1 multiply_bitcast_fusion
  4.4 0.5 collective-permute-start.4
  5.0 4.1 %collective-permute-start.5 = (f32[2,1,7,1024]{3,2,1,0:T(8,128)S(1)}, f32[2,1,7,1024]{3,2,1,0:T(8,128)S(1)}, u32[]{:S(2)}, u32[]{:S(2)}) collective-permute-start(f32[2,1,7,1024]{3,2,1,0:T(8,128)S(1)} %get-tuple-element.80), channel_id=1, source_target_pairs={{4,0},{8,4},{12,8},{16,12},{20,16},{24,20},{28,24},{0,28},{5,1},{9... | collective-permute-start | bytes 172040 | tf_op jit(solution)/shard_map/ppermute | solution.py:22
  9.7 3.5 %collective-permute-start.1 = (f32[3,7,1024]{2,1,0:T(8,128)S(1)}, f32[3,7,1024]{2,1,0:T(8,128)S(1)}, u32[]{:S(2)}, u32[]{:S(2)}) collective-permute-start(f32[3,7,1024]{2,1,0:T(8,128)S(1)} %get-tuple-element.52), channel_id=1, source_target_pairs={{4,0},{8,4},{12,8},{16,12},{20,16},{24,20},{28,24},{0,28},{5,1},{9... | collective-permute-start | bytes 258056 | tf_op jit(solution)/shard_map/ppermute | solution.py:22
  14.5 0.7 multiply_reduce_fusion.9
  16.0 3.4 %collective-permute-start.3 = (f32[3,46,7]{2,1,0:T(8,128)S(1)}, f32[3,46,7]{2,1,0:T(8,128)S(1)}, u32[]{:S(2)}, u32[]{:S(2)}) collective-permute-start(f32[3,46,7]{2,1,0:T(8,128)S(1)} %get-tuple-element.39), channel_id=1, source_target_pairs={{1,0},{2,1},{3,2},{0,3},{5,4},{6,5},{7,6},{4,7},{9,8},{10,9},{11,1... | collective-permute-start | bytes 11600 | tf_op jit(solution)/shard_map/ppermute | solution.py:22
  19.4 2.9 %collective-permute-start.7 = (f32[2,1,46,7]{3,2,1,0:T(8,128)S(1)}, f32[2,1,46,7]{3,2,1,0:T(8,128)S(1)}, u32[]{:S(2)}, u32[]{:S(2)}) collective-permute-start(f32[2,1,46,7]{3,2,1,0:T(8,128)S(1)} %get-tuple-element.53), channel_id=1, source_target_pairs={{1,0},{2,1},{3,2},{0,3},{5,4},{6,5},{7,6},{4,7},{9,8},{10,9},{11,1... | collective-permute-start | bytes 7736 | tf_op jit(solution)/shard_map/ppermute | solution.py:22
  22.4 1.8 %collective-permute-done.7 = f32[2,1,46,7]{3,2,1,0:T(8,128)S(1)} collective-permute-done((f32[2,1,46,7]{3,2,1,0:T(8,128)S(1)}, f32[2,1,46,7]{3,2,1,0:T(8,128)S(1)}, u32[]{:S(2)}, u32[]{:S(2)}) %collective-permute-start.7) | collective-permute-done | bytes 2608 | tf_op jit(solution)/shard_map/ppermute | solution.py:22
  24.2 3.2 %collective-permute-done.6 = f32[2,1,46,7]{3,2,1,0:T(8,128)S(1)} collective-permute-done((f32[2,1,46,7]{3,2,1,0:T(8,128)S(1)}, f32[2,1,46,7]{3,2,1,0:T(8,128)S(1)}, u32[]{:S(2)}, u32[]{:S(2)}) %collective-permute-start.6) | collective-permute-done | bytes 2608 | tf_op jit(solution)/shard_map/ppermute | solution.py:19
  29.7 0.5 fusion.16
  30.3 0.8 fusion.65
  31.6 0.7 slice_subtract_fusion.1
  32.3 0.8 fusion.64
  34.5 0.6 slice_subtract_fusion.9
  35.7 0.6 slice_subtract_fusion.8
  36.6 0.6 slice_subtract_fusion.7
  37.6 0.6 slice_subtract_fusion.6
  38.8 1.1 multiply_reduce_fusion.5
  39.9 0.9 multiply_reduce_fusion.11
  40.8 37.0 %psum.28 = f32[1]{0:T(128)} all-reduce(f32[1]{0:T(128)} %bitcast.29), channel_id=1, replica_groups=mesh['gx'=8,'gy'=4] {'gx','gy'}, use_global_device_ids=true, to_apply=%region_3.4 | all-reduce | flops 1 | bytes 8 | tf_op jit(solution)/shard_map/psum | solution.py:118
  78.5 0.7 multiply_reduce_fusion.4
  79.3 3.5 %collective-permute-start.9 = (f32[2,1,7,1024]{3,2,1,0:T(8,128)S(1)}, f32[2,1,7,1024]{3,2,1,0:T(8,128)S(1)}, u32[]{:S(2)}, u32[]{:S(2)}) collective-permute-start(f32[2,1,7,1024]{3,2,1,0:T(8,128)S(1)} %get-tuple-element.76), channel_id=1, source_target_pairs={{4,0},{8,4},{12,8},{16,12},{20,16},{24,20},{28,24},{0,28},{5,1},{9... | collective-permute-start | bytes 172040 | tf_op jit(solution)/shard_map/ppermute | solution.py:22
  82.8 0.7 fusion.63
  83.5 1.2 collective-permute-done.8
  84.9 2.5 %collective-permute-start.11 = (f32[2,1,46,7]{3,2,1,0:T(8,128)S(1)}, f32[2,1,46,7]{3,2,1,0:T(8,128)S(1)}, u32[]{:S(2)}, u32[]{:S(2)}) collective-permute-start(f32[2,1,46,7]{3,2,1,0:T(8,128)S(1)} %get-tuple-element.49), channel_id=1, source_target_pairs={{1,0},{2,1},{3,2},{0,3},{5,4},{6,5},{7,6},{4,7},{9,8},{10,9},{11,1... | collective-permute-start | bytes 7736 | tf_op jit(solution)/shard_map/ppermute | solution.py:22
  87.4 0.8 multiply_reduce_fusion.8
  88.1 5.1 %stack.171 = f32[8,1]{0,1:T(1,128)S(1)} concatenate(f32[1,1]{0,1:T(1,128)} %bitcast.35, f32[1,1]{0,1:T(1,128)} %bitcast.36, f32[1,1]{0,1:T(1,128)} %bitcast.37, f32[1,1]{0,1:T(1,128)} %bitcast.38, f32[1,1]{0,1:T(1,128)} %bitcast.39, f32[1,1]{0,1:T(1,128)} %bitcast.40, f32[1,1]{0,1:T(1,128)} %bitcast.41, f32[1,1]{0,1:T(1,128)} %bitcast.42), dimensions={0} | concatenate | bytes 64 | tf_op jit(solution)/shard_map/stack | solution.py:116
  93.3 0.6 copy-done.53
  93.9 1.1 concatenate.135
  95.5 0.8 fusion.62
  96.4 0.7 slice_subtract_fusion
  97.0 0.8 fusion.61
  97.9 0.6 slice_subtract_fusion.5
  98.4 0.8 fusion.60
  99.3 0.6 slice_subtract_fusion.4
  99.8 0.8 multiply_reduce_fusion.3
  100.7 0.6 slice_subtract_fusion.3
  101.6 0.6 copy-done.3
  102.5 0.6 slice_subtract_fusion.2
  103.6 1.0 multiply_reduce_fusion
  105.1 5.2 %stack.181 = f32[8,1]{0,1:T(1,128)S(1)} concatenate(f32[1,1]{0,1:T(1,128)} %bitcast.44, f32[1,1]{0,1:T(1,128)} %bitcast.45, f32[1,1]{0,1:T(1,128)} %bitcast.46, f32[1,1]{0,1:T(1,128)} %bitcast.47, f32[1,1]{0,1:T(1,128)} %bitcast.48, f32[1,1]{0,1:T(1,128)} %bitcast.49, f32[1,1]{0,1:T(1,128)} %bitcast.50, f32[1,1]{0,1:T(1,128)} %bitcast.51), dimensions={0} | concatenate | bytes 64 | tf_op jit(solution)/shard_map/stack | solution.py:116
  110.3 0.8 multiply_reduce_fusion.10
  111.1 40.4 %all-reduce = (f32[1]{0:T(128)}, f32[8,1]{0,1:T(1,128)S(1)}, f32[8,1]{0,1:T(1,128)S(1)}) all-reduce(f32[1]{0:T(128)} %bitcast.31, f32[8,1]{0,1:T(1,128)S(1)} %stack.181, f32[8,1]{0,1:T(1,128)S(1)} %stack.171), channel_id=1, replica_groups=mesh['gx'=8,'gy'=4] {'gx','gy'}, use_global_device_ids=true, to_apply=%region_5.6 | all-reduce | flops 17 | bytes 136 | tf_op jit(solution)/shard_map/psum | solution.py:118
  152.2 0.7 slice_bitcast_fusion.21
  153.0 0.6 pad_maximum_fusion.7
  (171 shorter events, 9.8 us)
Async XLA Ops:
  0.6 8.4 %copy-start.54 = (f32[16]{0:T(128)S(1)}, f32[16]{0:T(128)}, u32[]{:S(2)}) copy-start(f32[16]{0:T(128)} %param.13) | copy-start | bytes 196
  0.6 8.4 %copy-start.52 = (s32[32,1024]{1,0:T(8,128)S(1)}, s32[32,1024]{1,0:T(8,128)}, u32[]{:S(2)}) copy-start(s32[32,1024]{1,0:T(8,128)} %param.12) | copy-start | bytes 393220
  0.7 8.4 %copy-start.51 = (s32[32,1024]{1,0:T(8,128)S(1)}, s32[32,1024]{1,0:T(8,128)}, u32[]{:S(2)}) copy-start(s32[32,1024]{1,0:T(8,128)} %param.11) | copy-start | bytes 393220
  3.3 6.3 %copy-start.50 = (f32[32,1024]{1,0:T(8,128)S(1)}, f32[32,1024]{1,0:T(8,128)}, u32[]{:S(2)}) copy-start(f32[32,1024]{1,0:T(8,128)} %param.10) | copy-start | bytes 393220
  4.4 10.8 %collective-permute-start.4 = (f32[2,1,7,1024]{3,2,1,0:T(8,128)S(1)}, f32[2,1,7,1024]{3,2,1,0:T(8,128)S(1)}, u32[]{:S(2)}, u32[]{:S(2)}) collective-permute-start(f32[2,1,7,1024]{3,2,1,0:T(8,128)S(1)} %get-tuple-element.79), channel_id=1, source_target_pairs={{0,4},{4,8},{8,12},{12,16},{16,20},{20,24},{24,28},{28,0},{1,5},{5... | collective-permute-start | bytes 172040 | tf_op jit(solution)/shard_map/ppermute | solution.py:19
  5.0 10.3 %collective-permute-start.5 = (f32[2,1,7,1024]{3,2,1,0:T(8,128)S(1)}, f32[2,1,7,1024]{3,2,1,0:T(8,128)S(1)}, u32[]{:S(2)}, u32[]{:S(2)}) collective-permute-start(f32[2,1,7,1024]{3,2,1,0:T(8,128)S(1)} %get-tuple-element.80), channel_id=1, source_target_pairs={{4,0},{8,4},{12,8},{16,12},{20,16},{24,20},{28,24},{0,28},{5,1},{9... | collective-permute-start | bytes 172040 | tf_op jit(solution)/shard_map/ppermute | solution.py:22
  9.6 6.2 %collective-permute-start = (f32[3,7,1024]{2,1,0:T(8,128)S(1)}, f32[3,7,1024]{2,1,0:T(8,128)S(1)}, u32[]{:S(2)}, u32[]{:S(2)}) collective-permute-start(f32[3,7,1024]{2,1,0:T(8,128)S(1)} %get-tuple-element.51), channel_id=1, source_target_pairs={{0,4},{4,8},{8,12},{12,16},{16,20},{20,24},{24,28},{28,0},{1,5},{5... | collective-permute-start | bytes 258056 | tf_op jit(solution)/shard_map/ppermute | solution.py:19
  9.7 6.1 %collective-permute-start.1 = (f32[3,7,1024]{2,1,0:T(8,128)S(1)}, f32[3,7,1024]{2,1,0:T(8,128)S(1)}, u32[]{:S(2)}, u32[]{:S(2)}) collective-permute-start(f32[3,7,1024]{2,1,0:T(8,128)S(1)} %get-tuple-element.52), channel_id=1, source_target_pairs={{4,0},{8,4},{12,8},{16,12},{20,16},{24,20},{28,24},{0,28},{5,1},{9... | collective-permute-start | bytes 258056 | tf_op jit(solution)/shard_map/ppermute | solution.py:22
  16.0 11.6 %collective-permute-start.3 = (f32[3,46,7]{2,1,0:T(8,128)S(1)}, f32[3,46,7]{2,1,0:T(8,128)S(1)}, u32[]{:S(2)}, u32[]{:S(2)}) collective-permute-start(f32[3,46,7]{2,1,0:T(8,128)S(1)} %get-tuple-element.39), channel_id=1, source_target_pairs={{1,0},{2,1},{3,2},{0,3},{5,4},{6,5},{7,6},{4,7},{9,8},{10,9},{11,1... | collective-permute-start | bytes 11600 | tf_op jit(solution)/shard_map/ppermute | solution.py:22
  19.3 8.2 %collective-permute-start.2 = (f32[3,46,7]{2,1,0:T(8,128)S(1)}, f32[3,46,7]{2,1,0:T(8,128)S(1)}, u32[]{:S(2)}, u32[]{:S(2)}) collective-permute-start(f32[3,46,7]{2,1,0:T(8,128)S(1)} %get-tuple-element.40), channel_id=1, source_target_pairs={{0,1},{1,2},{2,3},{3,0},{4,5},{5,6},{6,7},{7,4},{8,9},{9,10},{10,1... | collective-permute-start | bytes 11600 | tf_op jit(solution)/shard_map/ppermute | solution.py:19
  19.4 4.7 %collective-permute-start.7 = (f32[2,1,46,7]{3,2,1,0:T(8,128)S(1)}, f32[2,1,46,7]{3,2,1,0:T(8,128)S(1)}, u32[]{:S(2)}, u32[]{:S(2)}) collective-permute-start(f32[2,1,46,7]{3,2,1,0:T(8,128)S(1)} %get-tuple-element.53), channel_id=1, source_target_pairs={{1,0},{2,1},{3,2},{0,3},{5,4},{6,5},{7,6},{4,7},{9,8},{10,9},{11,1... | collective-permute-start | bytes 7736 | tf_op jit(solution)/shard_map/ppermute | solution.py:22
  22.4 5.0 %collective-permute-start.6 = (f32[2,1,46,7]{3,2,1,0:T(8,128)S(1)}, f32[2,1,46,7]{3,2,1,0:T(8,128)S(1)}, u32[]{:S(2)}, u32[]{:S(2)}) collective-permute-start(f32[2,1,46,7]{3,2,1,0:T(8,128)S(1)} %get-tuple-element.54), channel_id=1, source_target_pairs={{0,1},{1,2},{2,3},{3,0},{4,5},{5,6},{6,7},{7,4},{8,9},{9,10},{10,1... | collective-permute-start | bytes 7736 | tf_op jit(solution)/shard_map/ppermute | solution.py:19
  33.3 4.3 %copy-start.2 = (f32[34,1026]{1,0:T(8,128)}, f32[34,1026]{1,0:T(8,128)S(1)}, u32[]{:S(2)}) copy-start(f32[34,1026]{1,0:T(8,128)S(1)} %slice.944) | copy-start | bytes 418612
  33.4 2.3 %copy-start.6 = (f32[38,1030]{1,0:T(8,128)}, f32[38,1030]{1,0:T(8,128)S(1)}, u32[]{:S(2)}) copy-start(f32[38,1030]{1,0:T(8,128)S(1)} %slice.914) | copy-start | bytes 469684
  33.6 3.0 %copy-start.4 = (f32[36,1028]{1,0:T(8,128)}, f32[36,1028]{1,0:T(8,128)S(1)}, u32[]{:S(2)}) copy-start(f32[36,1028]{1,0:T(8,128)S(1)} %slice.928) | copy-start | bytes 444100
  35.4 1.2 copy-start.18
  35.4 1.1 copy-start.20
  35.4 1.1 copy-start.22
  35.4 1.1 copy-start.24
  38.7 1.2 copy-start.42
  38.7 1.1 copy-start.44
  38.7 1.1 copy-start.46
  38.7 1.1 copy-start.48
  79.2 5.5 %collective-permute-start.8 = (f32[2,1,7,1024]{3,2,1,0:T(8,128)S(1)}, f32[2,1,7,1024]{3,2,1,0:T(8,128)S(1)}, u32[]{:S(2)}, u32[]{:S(2)}) collective-permute-start(f32[2,1,7,1024]{3,2,1,0:T(8,128)S(1)} %get-tuple-element.75), channel_id=1, source_target_pairs={{0,4},{4,8},{8,12},{12,16},{16,20},{20,24},{24,28},{28,0},{1,5},{5... | collective-permute-start | bytes 172040 | tf_op jit(solution)/shard_map/ppermute | solution.py:19
  79.3 5.5 %collective-permute-start.9 = (f32[2,1,7,1024]{3,2,1,0:T(8,128)S(1)}, f32[2,1,7,1024]{3,2,1,0:T(8,128)S(1)}, u32[]{:S(2)}, u32[]{:S(2)}) collective-permute-start(f32[2,1,7,1024]{3,2,1,0:T(8,128)S(1)} %get-tuple-element.76), channel_id=1, source_target_pairs={{4,0},{8,4},{12,8},{16,12},{20,16},{24,20},{28,24},{0,28},{5,1},{9... | collective-permute-start | bytes 172040 | tf_op jit(solution)/shard_map/ppermute | solution.py:22
  84.9 8.4 %collective-permute-start.11 = (f32[2,1,46,7]{3,2,1,0:T(8,128)S(1)}, f32[2,1,46,7]{3,2,1,0:T(8,128)S(1)}, u32[]{:S(2)}, u32[]{:S(2)}) collective-permute-start(f32[2,1,46,7]{3,2,1,0:T(8,128)S(1)} %get-tuple-element.49), channel_id=1, source_target_pairs={{1,0},{2,1},{3,2},{0,3},{5,4},{6,5},{7,6},{4,7},{9,8},{10,9},{11,1... | collective-permute-start | bytes 7736 | tf_op jit(solution)/shard_map/ppermute | solution.py:22
  87.4 6.5 %collective-permute-start.10 = (f32[2,1,46,7]{3,2,1,0:T(8,128)S(1)}, f32[2,1,46,7]{3,2,1,0:T(8,128)}, u32[]{:S(2)}, u32[]{:S(2)}) collective-permute-start(f32[2,1,46,7]{3,2,1,0:T(8,128)S(1)} %get-tuple-element.50), channel_id=1, source_target_pairs={{0,1},{1,2},{2,3},{3,0},{4,5},{5,6},{6,7},{7,4},{8,9},{9,10},{10,1... | collective-permute-start | bytes 7736 | tf_op jit(solution)/shard_map/ppermute | solution.py:19
  95.0 1.4 copy-start.1
  96.3 1.5 copy-start.9
  96.3 1.5 copy-start.11
  96.3 1.5 copy-start.13
  96.3 1.5 copy-start.15
  96.4 1.5 copy-start.17
  97.8 1.4 copy-start.7
  97.8 1.4 copy-start.35
  97.8 1.4 copy-start.37
  97.9 1.4 copy-start.39
  97.9 1.4 copy-start.41
  99.2 1.4 copy-start.5
  99.2 1.4 copy-start.19
  99.2 1.4 copy-start.21
  99.3 1.4 copy-start.23
  99.3 1.4 copy-start.25
  101.2 1.1 copy-start.29
  101.3 1.2 copy-start.31
  101.3 1.2 copy-start.33
  102.5 1.0 copy-start.47
  102.5 1.1 copy-start.49
  (19 other events, 16.0 us)
where the time goes:
time: 154 us
  blocking collectives  77.4 us (50%)
  other arithmetic  23.4 us (15%)
  local copies, waits for them, and re-layouts  21.2 us (14%)
  starting transfers between devices  20.6 us (13%)
  waiting for transfers between devices  6.73 us (4%)
  between operations  4.29 us (3%)
    psum x2, blocking collectives, per_device(): term_total, state_total = lax.psum((term_local, state_local), ('gx', 'gy'))  77.4 us
    ppermute x6, starting transfers between devices, padded(): lax.ppermute(lax.slice_in_dim(block, 0, width, axis=dim), axis, backward)  19.9 us
    another operation x2, local copies, waits for them, and re-layouts, per_device(): jnp.stack([jnp.sum(vector * vector, axis=(0, 2, 3)) for vector in chebysh...  10.4 us
    reduce_sum x12, other arithmetic, per_device(): jnp.sum(vector * vector, axis=(0, 2, 3))  9.75 us
    sub x10, other arithmetic, per_device(): following = 2.0 * applied - shrink(previous, previous_margin - margin + 1)  5.76 us
    ppermute x6, waiting for transfers between devices, padded(): lax.ppermute(lax.slice_in_dim(block, block.shape[dim] - width, None, axis...  4.9 us
    unnamed x110, local copies, waits for them, and re-layouts  3.2 us
  transfers between devices with their start and end apart: 12, of which 4 were waited for; matrix products, arithmetic and copies ran while one was open for 5% of the time, Pallas kernels for 0%

commit v1 on v0

--- a/solution.py
+++ b/solution.py
@@ -115,7 +115,7 @@
             accumulate = accumulate + weights[degree] * jnp.stack([real_rot, imag_rot])
         term_local = jnp.stack([jnp.sum(vector * vector, axis=(0, 2, 3)) for vector in chebyshev])
         state_local = jnp.sum(accumulate * accumulate, axis=(0, 2, 3))
-        term_total, state_total = lax.psum((term_local, state_local), ("gx", "gy"))
+        term_total, state_total = lax.psum(lax.psum((term_local, state_local), "gy"), "gx")
         norm_rows.append(term_total / cell_count)
         rescale = lax.rsqrt(state_total / cell_count + epsilon)
         packet_state = accumulate * rescale[None, :, None, None]

time: 154 us -> 123 us (0.80)
  blocking collectives: 77.4 us -> 48.3 us
  local copies, waits for them, and re-layouts: 21.2 us -> 19.6 us
    psum x2 -> x4, blocking collectives: 77.4 us -> 48.3 us  [the longest x2 29.4 us: per_device(): lax.psum(lax.psum((term_local, state_local), 'gy'), 'gx')]
    unnamed x110 -> x116, local copies, waits for them, and re-layouts: 3.2 us -> 2.61 us
  transfers between devices with their start and end apart: 12 -> 12, of which waited for: 4 -> 4; matrix products, arithmetic and copies ran while one was open for 5% -> 7% of each run, Pallas kernels for 0% -> 0%
where the time goes in v1:
time: 123 us; the launch traced here: 122 us
  blocking collectives  48.3 us (39%)
  other arithmetic  23.2 us (19%)
  starting transfers between devices  20.3 us (17%)
  local copies, waits for them, and re-layouts  19.6 us (16%)
  waiting for transfers between devices  6.77 us (6%)
  between operations  4.27 us (3%)
    psum x2, blocking collectives, per_device(): lax.psum(lax.psum((term_local, state_local), 'gy'), 'gx')  29.4 us
    ppermute x6, starting transfers between devices, padded(): lax.ppermute(lax.slice_in_dim(block, 0, width, axis=dim), axis, backward)  19.5 us
    psum x2, blocking collectives, per_device(): lax.psum((term_local, state_local), 'gy')  18.9 us
    another operation x2, local copies, waits for them, and re-layouts, per_device(): jnp.stack([jnp.sum(vector * vector, axis=(0, 2, 3)) for vector in chebysh...  10.2 us
    reduce_sum x12, other arithmetic, per_device(): jnp.sum(vector * vector, axis=(0, 2, 3))  9.57 us
    sub x10, other arithmetic, per_device(): following = 2.0 * applied - shrink(previous, previous_margin - margin + 1)  5.79 us
    ppermute x6, waiting for transfers between devices, padded(): lax.ppermute(lax.slice_in_dim(block, block.shape[dim] - width, None, axis...  4.94 us
    unnamed x116, local copies, waits for them, and re-layouts  2.61 us
  transfers between devices with their start and end apart: 12, of which 4 were waited for; matrix products, arithmetic and copies ran while one was open for 7% of the time, Pallas kernels for 0%

profile of v1, /device:TPU:0, one launch (start us, length us, event | category | flops | bytes accessed | tf_op | source)
XLA Modules:
  0.0 122.5 jit_solution(7601375204090458591)
XLA Ops:
  0.7 1.3 %fusion.128 = (s32[1,1]{1,0:T(1,128)}, s32[1,1]{1,0:T(1,128)}) fusion(s32[1,2]{1,0:T(1,128)} %param.14), kind=kLoop, calls=%fused_computation.302 | loop fusion | bytes 16 | tf_op jit(solution)/shard_map/slice | solution.py:89
  2.0 0.7 fusion.100
  2.6 0.7 fusion.97
  3.3 1.1 multiply_bitcast_fusion
  5.0 4.1 %collective-permute-start.5 = (f32[2,1,7,1024]{3,2,1,0:T(8,128)S(1)}, f32[2,1,7,1024]{3,2,1,0:T(8,128)S(1)}, u32[]{:S(2)}, u32[]{:S(2)}) collective-permute-start(f32[2,1,7,1024]{3,2,1,0:T(8,128)S(1)} %get-tuple-element.83), channel_id=1, source_target_pairs={{4,0},{8,4},{12,8},{16,12},{20,16},{24,20},{28,24},{0,28},{5,1},{9... | collective-permute-start | bytes 172040 | tf_op jit(solution)/shard_map/ppermute | solution.py:22
  9.7 3.5 %collective-permute-start.1 = (f32[3,7,1024]{2,1,0:T(8,128)S(1)}, f32[3,7,1024]{2,1,0:T(8,128)S(1)}, u32[]{:S(2)}, u32[]{:S(2)}) collective-permute-start(f32[3,7,1024]{2,1,0:T(8,128)S(1)} %get-tuple-element.55), channel_id=1, source_target_pairs={{4,0},{8,4},{12,8},{16,12},{20,16},{24,20},{28,24},{0,28},{5,1},{9... | collective-permute-start | bytes 258056 | tf_op jit(solution)/shard_map/ppermute | solution.py:22
  14.5 0.6 multiply_reduce_fusion.9
  15.2 0.6 collective-permute-done
  16.0 3.4 %collective-permute-start.3 = (f32[3,46,7]{2,1,0:T(8,128)S(1)}, f32[3,46,7]{2,1,0:T(8,128)S(1)}, u32[]{:S(2)}, u32[]{:S(2)}) collective-permute-start(f32[3,46,7]{2,1,0:T(8,128)S(1)} %get-tuple-element.42), channel_id=1, source_target_pairs={{1,0},{2,1},{3,2},{0,3},{5,4},{6,5},{7,6},{4,7},{9,8},{10,9},{11,1... | collective-permute-start | bytes 11600 | tf_op jit(solution)/shard_map/ppermute | solution.py:22
  19.4 2.9 %collective-permute-start.7 = (f32[2,1,46,7]{3,2,1,0:T(8,128)S(1)}, f32[2,1,46,7]{3,2,1,0:T(8,128)S(1)}, u32[]{:S(2)}, u32[]{:S(2)}) collective-permute-start(f32[2,1,46,7]{3,2,1,0:T(8,128)S(1)} %get-tuple-element.56), channel_id=1, source_target_pairs={{1,0},{2,1},{3,2},{0,3},{5,4},{6,5},{7,6},{4,7},{9,8},{10,9},{11,1... | collective-permute-start | bytes 7736 | tf_op jit(solution)/shard_map/ppermute | solution.py:22
  22.4 1.8 %collective-permute-done.7 = f32[2,1,46,7]{3,2,1,0:T(8,128)S(1)} collective-permute-done((f32[2,1,46,7]{3,2,1,0:T(8,128)S(1)}, f32[2,1,46,7]{3,2,1,0:T(8,128)S(1)}, u32[]{:S(2)}, u32[]{:S(2)}) %collective-permute-start.7) | collective-permute-done | bytes 2608 | tf_op jit(solution)/shard_map/ppermute | solution.py:22
  24.2 3.2 %collective-permute-done.6 = f32[2,1,46,7]{3,2,1,0:T(8,128)S(1)} collective-permute-done((f32[2,1,46,7]{3,2,1,0:T(8,128)S(1)}, f32[2,1,46,7]{3,2,1,0:T(8,128)S(1)}, u32[]{:S(2)}, u32[]{:S(2)}) %collective-permute-start.6) | collective-permute-done | bytes 2608 | tf_op jit(solution)/shard_map/ppermute | solution.py:19
  30.3 0.8 fusion.65
  32.3 0.7 slice_subtract_fusion.1
  33.5 0.6 slice_subtract_fusion.9
  35.0 0.6 slice_subtract_fusion.8
  35.8 0.6 slice_subtract_fusion.7
  36.8 0.6 slice_subtract_fusion.6
  38.0 1.1 multiply_reduce_fusion.5
  39.2 0.9 multiply_reduce_fusion.11
  40.0 8.1 %psum.56 = f32[1]{0:T(128)} all-reduce(f32[1]{0:T(128)} %bitcast.29), channel_id=1, replica_groups=mesh['gx'=8,'gy'=4] {'gy'}, use_global_device_ids=true, to_apply=%region_3.4 | all-reduce | flops 1 | bytes 8 | tf_op jit(solution)/shard_map/psum | solution.py:118
  48.1 0.7 fusion.64
  48.8 14.2 %psum.57 = f32[1]{0:T(128)} all-reduce(f32[1]{0:T(128)} %psum.56), channel_id=1, replica_groups=mesh['gx'=8,'gy'=4] {'gx'}, use_global_device_ids=true, to_apply=%region_4.5 | all-reduce | flops 1 | bytes 8 | tf_op jit(solution)/shard_map/psum | solution.py:118
  63.7 0.7 multiply_reduce_fusion.4
  64.5 3.5 %collective-permute-start.9 = (f32[2,1,7,1024]{3,2,1,0:T(8,128)S(1)}, f32[2,1,7,1024]{3,2,1,0:T(8,128)S(1)}, u32[]{:S(2)}, u32[]{:S(2)}) collective-permute-start(f32[2,1,7,1024]{3,2,1,0:T(8,128)S(1)} %get-tuple-element.79), channel_id=1, source_target_pairs={{4,0},{8,4},{12,8},{16,12},{20,16},{24,20},{28,24},{0,28},{5,1},{9... | collective-permute-start | bytes 172040 | tf_op jit(solution)/shard_map/ppermute | solution.py:22
  68.0 0.8 fusion.63
  68.8 1.2 collective-permute-done.8
  70.1 2.0 %collective-permute-start.11 = (f32[2,1,46,7]{3,2,1,0:T(8,128)S(1)}, f32[2,1,46,7]{3,2,1,0:T(8,128)S(1)}, u32[]{:S(2)}, u32[]{:S(2)}) collective-permute-start(f32[2,1,46,7]{3,2,1,0:T(8,128)S(1)} %get-tuple-element.52), channel_id=1, source_target_pairs={{1,0},{2,1},{3,2},{0,3},{5,4},{6,5},{7,6},{4,7},{9,8},{10,9},{11,1... | collective-permute-start | bytes 7736 | tf_op jit(solution)/shard_map/ppermute | solution.py:22
  72.3 0.7 multiply_reduce_fusion.8
  73.1 5.1 %stack.171 = f32[8,1]{0,1:T(1,128)S(1)} concatenate(f32[1,1]{0,1:T(1,128)} %bitcast.35, f32[1,1]{0,1:T(1,128)} %bitcast.36, f32[1,1]{0,1:T(1,128)} %bitcast.37, f32[1,1]{0,1:T(1,128)} %bitcast.38, f32[1,1]{0,1:T(1,128)} %bitcast.39, f32[1,1]{0,1:T(1,128)} %bitcast.40, f32[1,1]{0,1:T(1,128)} %bitcast.41, f32[1,1]{0,1:T(1,128)} %bitcast.42), dimensions={0} | concatenate | bytes 64 | tf_op jit(solution)/shard_map/stack | solution.py:116
  78.4 0.5 fusion.6
  79.0 0.7 fusion.62
  79.7 0.7 slice_subtract_fusion
  80.4 0.8 fusion.61
  81.3 0.6 slice_subtract_fusion.5
  81.8 0.8 fusion.60
  82.7 0.6 slice_subtract_fusion.4
  83.2 0.8 multiply_reduce_fusion.3
  84.0 0.6 slice_subtract_fusion.3
  84.9 0.6 copy-done.7
  85.9 0.6 slice_subtract_fusion.2
  87.0 1.0 multiply_reduce_fusion
  88.5 5.2 %stack.181 = f32[8,1]{0,1:T(1,128)S(1)} concatenate(f32[1,1]{0,1:T(1,128)} %bitcast.44, f32[1,1]{0,1:T(1,128)} %bitcast.45, f32[1,1]{0,1:T(1,128)} %bitcast.46, f32[1,1]{0,1:T(1,128)} %bitcast.47, f32[1,1]{0,1:T(1,128)} %bitcast.48, f32[1,1]{0,1:T(1,128)} %bitcast.49, f32[1,1]{0,1:T(1,128)} %bitcast.50, f32[1,1]{0,1:T(1,128)} %bitcast.51), dimensions={0} | concatenate | bytes 64 | tf_op jit(solution)/shard_map/stack | solution.py:116
  93.6 0.8 multiply_reduce_fusion.10
  94.5 10.8 %all-reduce.1 = (f32[1]{0:T(128)}, f32[8,1]{0,1:T(1,128)S(1)}, f32[8,1]{0,1:T(1,128)S(1)}) all-reduce(f32[1]{0:T(128)} %bitcast.31, f32[8,1]{0,1:T(1,128)S(1)} %stack.181, f32[8,1]{0,1:T(1,128)S(1)} %stack.171), channel_id=1, replica_groups=mesh['gx'=8,'gy'=4] {'gy'}, use_global_device_ids=true, to_apply=%region_6.7 | all-reduce | flops 17 | bytes 136 | tf_op jit(solution)/shard_map/psum | solution.py:118
  105.3 15.2 %all-reduce = (f32[1]{0:T(128)}, f32[8,1]{0,1:T(1,128)S(1)}, f32[8,1]{0,1:T(1,128)S(1)}) all-reduce(f32[1]{0:T(128)} %get-tuple-element.8, f32[8,1]{0,1:T(1,128)S(1)} %get-tuple-element.9, f32[8,1]{0,1:T(1,128)S(1)} %get-tuple-element.10), channel_id=1, replica_groups=mesh['gx'=8,'gy'=4] {'gx'}, use_global_device_ids=true, to_apply=%region_7.8 | all-reduce | flops 17 | bytes 136 | tf_op jit(solution)/shard_map/psum | solution.py:118
  121.2 0.7 slice_bitcast_fusion.21
  121.9 0.6 pad_maximum_fusion.7
  (179 shorter events, 10.3 us)
Async XLA Ops:
  0.6 8.4 %copy-start.57 = (f32[16]{0:T(128)S(1)}, f32[16]{0:T(128)}, u32[]{:S(2)}) copy-start(f32[16]{0:T(128)} %param.13) | copy-start | bytes 196
  0.6 8.4 %copy-start.56 = (s32[32,1024]{1,0:T(8,128)S(1)}, s32[32,1024]{1,0:T(8,128)}, u32[]{:S(2)}) copy-start(s32[32,1024]{1,0:T(8,128)} %param.12) | copy-start | bytes 393220
  0.7 8.4 %copy-start.55 = (s32[32,1024]{1,0:T(8,128)S(1)}, s32[32,1024]{1,0:T(8,128)}, u32[]{:S(2)}) copy-start(s32[32,1024]{1,0:T(8,128)} %param.11) | copy-start | bytes 393220
  3.3 6.3 %copy-start.54 = (f32[32,1024]{1,0:T(8,128)S(1)}, f32[32,1024]{1,0:T(8,128)}, u32[]{:S(2)}) copy-start(f32[32,1024]{1,0:T(8,128)} %param.10) | copy-start | bytes 393220
  4.4 10.7 %collective-permute-start.4 = (f32[2,1,7,1024]{3,2,1,0:T(8,128)S(1)}, f32[2,1,7,1024]{3,2,1,0:T(8,128)S(1)}, u32[]{:S(2)}, u32[]{:S(2)}) collective-permute-start(f32[2,1,7,1024]{3,2,1,0:T(8,128)S(1)} %get-tuple-element.82), channel_id=1, source_target_pairs={{0,4},{4,8},{8,12},{12,16},{16,20},{20,24},{24,28},{28,0},{1,5},{5... | collective-permute-start | bytes 172040 | tf_op jit(solution)/shard_map/ppermute | solution.py:19
  5.0 10.2 %collective-permute-start.5 = (f32[2,1,7,1024]{3,2,1,0:T(8,128)S(1)}, f32[2,1,7,1024]{3,2,1,0:T(8,128)S(1)}, u32[]{:S(2)}, u32[]{:S(2)}) collective-permute-start(f32[2,1,7,1024]{3,2,1,0:T(8,128)S(1)} %get-tuple-element.83), channel_id=1, source_target_pairs={{4,0},{8,4},{12,8},{16,12},{20,16},{24,20},{28,24},{0,28},{5,1},{9... | collective-permute-start | bytes 172040 | tf_op jit(solution)/shard_map/ppermute | solution.py:22
  9.6 6.2 %collective-permute-start = (f32[3,7,1024]{2,1,0:T(8,128)S(1)}, f32[3,7,1024]{2,1,0:T(8,128)S(1)}, u32[]{:S(2)}, u32[]{:S(2)}) collective-permute-start(f32[3,7,1024]{2,1,0:T(8,128)S(1)} %get-tuple-element.54), channel_id=1, source_target_pairs={{0,4},{4,8},{8,12},{12,16},{16,20},{20,24},{24,28},{28,0},{1,5},{5... | collective-permute-start | bytes 258056 | tf_op jit(solution)/shard_map/ppermute | solution.py:19
  9.7 6.1 %collective-permute-start.1 = (f32[3,7,1024]{2,1,0:T(8,128)S(1)}, f32[3,7,1024]{2,1,0:T(8,128)S(1)}, u32[]{:S(2)}, u32[]{:S(2)}) collective-permute-start(f32[3,7,1024]{2,1,0:T(8,128)S(1)} %get-tuple-element.55), channel_id=1, source_target_pairs={{4,0},{8,4},{12,8},{16,12},{20,16},{24,20},{28,24},{0,28},{5,1},{9... | collective-permute-start | bytes 258056 | tf_op jit(solution)/shard_map/ppermute | solution.py:22
  16.0 11.6 %collective-permute-start.3 = (f32[3,46,7]{2,1,0:T(8,128)S(1)}, f32[3,46,7]{2,1,0:T(8,128)S(1)}, u32[]{:S(2)}, u32[]{:S(2)}) collective-permute-start(f32[3,46,7]{2,1,0:T(8,128)S(1)} %get-tuple-element.42), channel_id=1, source_target_pairs={{1,0},{2,1},{3,2},{0,3},{5,4},{6,5},{7,6},{4,7},{9,8},{10,9},{11,1... | collective-permute-start | bytes 11600 | tf_op jit(solution)/shard_map/ppermute | solution.py:22
  19.3 8.3 %collective-permute-start.2 = (f32[3,46,7]{2,1,0:T(8,128)S(1)}, f32[3,46,7]{2,1,0:T(8,128)S(1)}, u32[]{:S(2)}, u32[]{:S(2)}) collective-permute-start(f32[3,46,7]{2,1,0:T(8,128)S(1)} %get-tuple-element.43), channel_id=1, source_target_pairs={{0,1},{1,2},{2,3},{3,0},{4,5},{5,6},{6,7},{7,4},{8,9},{9,10},{10,1... | collective-permute-start | bytes 11600 | tf_op jit(solution)/shard_map/ppermute | solution.py:19
  19.4 4.7 %collective-permute-start.7 = (f32[2,1,46,7]{3,2,1,0:T(8,128)S(1)}, f32[2,1,46,7]{3,2,1,0:T(8,128)S(1)}, u32[]{:S(2)}, u32[]{:S(2)}) collective-permute-start(f32[2,1,46,7]{3,2,1,0:T(8,128)S(1)} %get-tuple-element.56), channel_id=1, source_target_pairs={{1,0},{2,1},{3,2},{0,3},{5,4},{6,5},{7,6},{4,7},{9,8},{10,9},{11,1... | collective-permute-start | bytes 7736 | tf_op jit(solution)/shard_map/ppermute | solution.py:22
  22.4 5.0 %collective-permute-start.6 = (f32[2,1,46,7]{3,2,1,0:T(8,128)S(1)}, f32[2,1,46,7]{3,2,1,0:T(8,128)S(1)}, u32[]{:S(2)}, u32[]{:S(2)}) collective-permute-start(f32[2,1,46,7]{3,2,1,0:T(8,128)S(1)} %get-tuple-element.57), channel_id=1, source_target_pairs={{0,1},{1,2},{2,3},{3,0},{4,5},{5,6},{6,7},{7,4},{8,9},{9,10},{10,1... | collective-permute-start | bytes 7736 | tf_op jit(solution)/shard_map/ppermute | solution.py:19
  31.4 5.4 %copy-start.6 = (f32[34,1026]{1,0:T(8,128)}, f32[34,1026]{1,0:T(8,128)S(1)}, u32[]{:S(2)}) copy-start(f32[34,1026]{1,0:T(8,128)S(1)} %slice.944) | copy-start | bytes 418612
  31.5 3.4 %copy-start.10 = (f32[38,1030]{1,0:T(8,128)}, f32[38,1030]{1,0:T(8,128)S(1)}, u32[]{:S(2)}) copy-start(f32[38,1030]{1,0:T(8,128)S(1)} %slice.914) | copy-start | bytes 469684
  31.6 4.1 %copy-start.8 = (f32[36,1028]{1,0:T(8,128)}, f32[36,1028]{1,0:T(8,128)S(1)}, u32[]{:S(2)}) copy-start(f32[36,1028]{1,0:T(8,128)S(1)} %slice.928) | copy-start | bytes 444100
  31.8 6.3 %copy-start.44 = (f32[32,1024]{1,0:T(8,128)}, f32[32,1024]{1,0:T(8,128)S(1)}, u32[]{:S(2)}) copy-start(f32[32,1024]{1,0:T(8,128)S(1)} %slice.960) | copy-start | bytes 393220
  31.9 1.6 %copy-start.12 = (f32[40,1032]{1,0:T(8,128)}, f32[40,1032]{1,0:T(8,128)S(1)}, u32[]{:S(2)}) copy-start(f32[40,1032]{1,0:T(8,128)S(1)} %slice.898) | copy-start | bytes 495364
  34.6 1.1 copy-start.20
  34.7 1.1 copy-start.22
  34.7 1.1 copy-start.24
  38.0 1.2 copy-start.46
  38.0 1.2 copy-start.48
  38.0 1.1 copy-start.50
  38.0 1.1 copy-start.52
  64.4 5.5 %collective-permute-start.8 = (f32[2,1,7,1024]{3,2,1,0:T(8,128)S(1)}, f32[2,1,7,1024]{3,2,1,0:T(8,128)S(1)}, u32[]{:S(2)}, u32[]{:S(2)}) collective-permute-start(f32[2,1,7,1024]{3,2,1,0:T(8,128)S(1)} %get-tuple-element.78), channel_id=1, source_target_pairs={{0,4},{4,8},{8,12},{12,16},{16,20},{20,24},{24,28},{28,0},{1,5},{5... | collective-permute-start | bytes 172040 | tf_op jit(solution)/shard_map/ppermute | solution.py:19
  64.5 5.5 %collective-permute-start.9 = (f32[2,1,7,1024]{3,2,1,0:T(8,128)S(1)}, f32[2,1,7,1024]{3,2,1,0:T(8,128)S(1)}, u32[]{:S(2)}, u32[]{:S(2)}) collective-permute-start(f32[2,1,7,1024]{3,2,1,0:T(8,128)S(1)} %get-tuple-element.79), channel_id=1, source_target_pairs={{4,0},{8,4},{12,8},{16,12},{20,16},{24,20},{28,24},{0,28},{5,1},{9... | collective-permute-start | bytes 172040 | tf_op jit(solution)/shard_map/ppermute | solution.py:22
  70.1 8.0 %collective-permute-start.11 = (f32[2,1,46,7]{3,2,1,0:T(8,128)S(1)}, f32[2,1,46,7]{3,2,1,0:T(8,128)S(1)}, u32[]{:S(2)}, u32[]{:S(2)}) collective-permute-start(f32[2,1,46,7]{3,2,1,0:T(8,128)S(1)} %get-tuple-element.52), channel_id=1, source_target_pairs={{1,0},{2,1},{3,2},{0,3},{5,4},{6,5},{7,6},{4,7},{9,8},{10,9},{11,1... | collective-permute-start | bytes 7736 | tf_op jit(solution)/shard_map/ppermute | solution.py:22
  72.1 6.0 %collective-permute-start.10 = (f32[2,1,46,7]{3,2,1,0:T(8,128)S(1)}, f32[2,1,46,7]{3,2,1,0:T(8,128)S(1)}, u32[]{:S(2)}, u32[]{:S(2)}) collective-permute-start(f32[2,1,46,7]{3,2,1,0:T(8,128)S(1)} %get-tuple-element.53), channel_id=1, source_target_pairs={{0,1},{1,2},{2,3},{3,0},{4,5},{5,6},{6,7},{7,4},{8,9},{9,10},{10,1... | collective-permute-start | bytes 7736 | tf_op jit(solution)/shard_map/ppermute | solution.py:19
  78.4 1.3 %copy-start.1 = (f32[42,1034]{1,0:T(8,128)S(1)}, f32[42,1034]{1,0:T(8,128)}, u32[]{:S(2)}) copy-start(f32[42,1034]{1,0:T(8,128)} %copy-done) | copy-start | bytes 521140
  78.4 1.3 %copy-start.3 = (f32[42,1034]{1,0:T(8,128)S(1)}, f32[42,1034]{1,0:T(8,128)}, u32[]{:S(2)}) copy-start(f32[42,1034]{1,0:T(8,128)} %copy-done.2) | copy-start | bytes 521140
  78.4 1.3 %copy-start.5 = (f32[42,1034]{1,0:T(8,128)S(1)}, f32[42,1034]{1,0:T(8,128)}, u32[]{:S(2)}) copy-start(f32[42,1034]{1,0:T(8,128)} %copy-done.4) | copy-start | bytes 521140
  79.7 1.5 %copy-start.13 = (f32[40,1032]{1,0:T(8,128)S(1)}, f32[40,1032]{1,0:T(8,128)}, u32[]{:S(2)}) copy-start(f32[40,1032]{1,0:T(8,128)} %copy-done.12) | copy-start | bytes 495364
  79.7 1.5 %copy-start.15 = (f32[40,1032]{1,0:T(8,128)S(1)}, f32[40,1032]{1,0:T(8,128)}, u32[]{:S(2)}) copy-start(f32[40,1032]{1,0:T(8,128)} %copy-done.14) | copy-start | bytes 495364
  79.7 1.5 %copy-start.17 = (f32[40,1032]{1,0:T(8,128)S(1)}, f32[40,1032]{1,0:T(8,128)}, u32[]{:S(2)}) copy-start(f32[40,1032]{1,0:T(8,128)} %copy-done.16) | copy-start | bytes 495364
  79.7 1.5 %copy-start.19 = (f32[40,1032]{1,0:T(8,128)S(1)}, f32[40,1032]{1,0:T(8,128)}, u32[]{:S(2)}) copy-start(f32[40,1032]{1,0:T(8,128)} %copy-done.18) | copy-start | bytes 495364
  81.2 1.4 %copy-start.11 = (f32[38,1030]{1,0:T(8,128)S(1)}, f32[38,1030]{1,0:T(8,128)}, u32[]{:S(2)}) copy-start(f32[38,1030]{1,0:T(8,128)} %copy-done.10) | copy-start | bytes 469684
  81.2 1.4 %copy-start.37 = (f32[38,1030]{1,0:T(8,128)S(1)}, f32[38,1030]{1,0:T(8,128)}, u32[]{:S(2)}) copy-start(f32[38,1030]{1,0:T(8,128)} %copy-done.36) | copy-start | bytes 469684
  81.2 1.4 %copy-start.39 = (f32[38,1030]{1,0:T(8,128)S(1)}, f32[38,1030]{1,0:T(8,128)}, u32[]{:S(2)}) copy-start(f32[38,1030]{1,0:T(8,128)} %copy-done.38) | copy-start | bytes 469684
  81.2 1.4 %copy-start.41 = (f32[38,1030]{1,0:T(8,128)S(1)}, f32[38,1030]{1,0:T(8,128)}, u32[]{:S(2)}) copy-start(f32[38,1030]{1,0:T(8,128)} %copy-done.40) | copy-start | bytes 469684
  81.2 1.4 %copy-start.43 = (f32[38,1030]{1,0:T(8,128)S(1)}, f32[38,1030]{1,0:T(8,128)}, u32[]{:S(2)}) copy-start(f32[38,1030]{1,0:T(8,128)} %copy-done.42) | copy-start | bytes 469684
  82.6 1.4 %copy-start.9 = (f32[36,1028]{1,0:T(8,128)S(1)}, f32[36,1028]{1,0:T(8,128)}, u32[]{:S(2)}) copy-start(f32[36,1028]{1,0:T(8,128)} %copy-done.8) | copy-start | bytes 444100
  82.6 1.4 %copy-start.21 = (f32[36,1028]{1,0:T(8,128)S(1)}, f32[36,1028]{1,0:T(8,128)}, u32[]{:S(2)}) copy-start(f32[36,1028]{1,0:T(8,128)} %copy-done.20) | copy-start | bytes 444100
  82.6 1.4 %copy-start.23 = (f32[36,1028]{1,0:T(8,128)S(1)}, f32[36,1028]{1,0:T(8,128)}, u32[]{:S(2)}) copy-start(f32[36,1028]{1,0:T(8,128)} %copy-done.22) | copy-start | bytes 444100
  82.6 1.4 %copy-start.25 = (f32[36,1028]{1,0:T(8,128)S(1)}, f32[36,1028]{1,0:T(8,128)}, u32[]{:S(2)}) copy-start(f32[36,1028]{1,0:T(8,128)} %copy-done.24) | copy-start | bytes 444100
  82.7 1.4 %copy-start.27 = (f32[36,1028]{1,0:T(8,128)S(1)}, f32[36,1028]{1,0:T(8,128)}, u32[]{:S(2)}) copy-start(f32[36,1028]{1,0:T(8,128)} %copy-done.26) | copy-start | bytes 444100
  84.6 1.2 copy-start.33
  84.6 1.2 copy-start.35
  85.9 1.2 copy-start.53
  (22 other events, 18.8 us)
